TPU v7x, 128 devices: a whole 4x4x4 slice. The times are simulated.
128 devices in a mesh: row: 8 (over x, core), col: 16 (over z, y).
Axes of the slice: x: 4, y: 4, z: 4, core: 2. Of those that a mesh axis runs over, the one named last changes fastest.
Arguments:
- tiles: bfloat16 [8, 16, 384, 128, 128], P('row', 'col'), may hold values from -0.15625 to 0.15625
- tile_row: int32 [8, 16, 384], P('row', 'col'), may hold values from 0 to 511, as said below
- tile_col: int32 [8, 16, 384], P('row', 'col'), may hold values from 0 to 255
- tile_count: int32 [8, 16], P('row', 'col'), may hold values from 96 to 384, as said below
- vectors: bfloat16 [32, 8, 16, 4096], P(None, 'row', 'col'), may hold values from -6 to 6
Outputs:
- image: bfloat16 [32, 524288], P(None, ('row', 'col'))
- back_image: bfloat16 [32, 8, 16, 4096], P(None, 'row', 'col')
Inputs may be any that keep to these rules, and one draw needn't show every extreme that they name: `tile_count`: some device has exactly 384 live slots. `tile_row`: the slots of each device, live or not, name exactly 12 distinct block rows in each aligned run of 32 block rows.
All inputs are finite; a program needn't handle non-finite values.
Results may differ from a plain program's by a relative error of at most 0.0041.
Values may be sent and summed in bfloat16 or wider, within the bound.
No kernel may reach another device: no remote copies, remote signals or barrier semaphores. Data moves between devices by JAX's collectives and lax.ppermute only.
A program may use at most 128 MiB of HBM per device.

v0:
```python
import jax
import jax.numpy as jnp
from jax import lax
from jax.sharding import PartitionSpec as P


def per_device(tiles, tile_row, tile_col, tile_count, vectors):
    vec_cols = vectors.shape[0]
    tile_size = tiles.shape[-1]
    slot_count = tiles.shape[2]
    local_tiles = tiles[0, 0]
    rows_local = tile_row[0, 0]
    cols_local = tile_col[0, 0]
    live_count = tile_count[0, 0]
    live_mask = (jnp.arange(slot_count, dtype=jnp.int32) < live_count).astype(jnp.float32)
    row_devices = lax.axis_size("row")
    col_devices = lax.axis_size("col")
    gathered = lax.all_gather(vectors, "row", axis=1, tiled=True)
    blk_cols = gathered.shape[1] * gathered.shape[3] // tile_size
    blk_rows = blk_cols * col_devices // row_devices
    col_vectors = gathered.reshape(vec_cols, blk_cols, tile_size)

    def slot_group():
        return (local_tiles, rows_local, cols_local, live_mask)

    def forward_terms(totals, start_slot, group_size):
        tile_block, row_index, col_index, slot_mask = slot_group()
        picked = jnp.take(col_vectors, col_index, axis=1)
        product = jnp.einsum("ksj,sij->ksi", picked, tile_block, preferred_element_type=jnp.float32)
        return totals.at[:, row_index].add(product * slot_mask[None, :, None])

    def sweep(term_fn, totals_zero):
        return term_fn(totals_zero, 0, slot_count)

    forward_sum = sweep(forward_terms, jnp.zeros((vec_cols, blk_rows, tile_size), jnp.float32))
    partial_rows = forward_sum.reshape(vec_cols, blk_rows * tile_size)
    share_sum = lax.psum_scatter(partial_rows, "col", scatter_dimension=1, tiled=True)
    image = share_sum.astype(jnp.bfloat16)
    row_image = lax.all_gather(image, "col", axis=1, tiled=True)
    row_blocks = row_image.reshape(vec_cols, blk_rows, tile_size)

    def backward_terms(totals, start_slot, group_size):
        tile_block, row_index, col_index, slot_mask = slot_group()
        picked = jnp.take(row_blocks, row_index, axis=1)
        product = jnp.einsum("ksi,sij->ksj", picked, tile_block, preferred_element_type=jnp.float32)
        return totals.at[:, col_index].add(product * slot_mask[None, :, None])

    backward_sum = sweep(backward_terms, jnp.zeros((vec_cols, blk_cols, tile_size), jnp.float32))
    partial_cols = backward_sum.reshape(vec_cols, row_devices, 1, vectors.shape[3])
    back_sum = lax.psum_scatter(partial_cols, "row", scatter_dimension=1, tiled=True)
    return (image, back_sum.astype(jnp.bfloat16))


def solution(mesh):
    return jax.shard_map(
        per_device,
        mesh=mesh,
        in_specs=(
            P("row", "col", None, None, None),
            P("row", "col", None),
            P("row", "col", None),
            P("row", "col"),
            P(None, "row", "col", None),
        ),
        out_specs=(P(None, ("row", "col")), P(None, "row", "col", None)),
        check_vma=False,
    )
```

profile of v0, /device:TPU:0, one launch (start us, length us, event | category | flops | bytes accessed | tf_op | source)
XLA Modules:
  0.0 400.8 jit_solution(5015955300966419793)
XLA Ops:
  7.2 0.0 all-gather.3.cloned.1.call-start
  7.2 0.7 all-gather.3.cloned.1.call-update
  7.9 0.0 reduce-scatter.3.cloned.1.call-start
  8.6 0.7 reduce.1
  9.3 0.7 fusion.22
  10.0 0.7 fusion.21
  10.7 26.6 %all-gather.3.cloned.1.call-done = bf16[32,8,1,4096]{3,0,2,1:T(8,128)(2,1)} async-done(((bf16[32,1,1,4096]{3,0,2,1:T(8,128)(2,1)}), bf16[32,8,1,4096]{3,0,2,1:T(8,128)(2,1)}) %all-gather.3.cloned.1.call-update) | async-done | bytes 2097168 | tf_op jit(solution)/shard_map/all_gather | solution.py:18
  37.3 2.7 copy.18
  40.1 2.4 reshape.89
  42.5 2.9 copy.19
  45.4 3.2 gather_fusion
  48.6 14.9 %broadcast_multiply_fusion.1 = f32[384,32,128]{2,1,0:T(8,128)} fusion(f32[384]{0:T(512)S(1)} %get-tuple-element.6, bf16[1,1,384,128,128]{4,3,2,1,0:T(8,128)(2,1)} %param.5, bf16[384,32,128]{2,1,0:T(8,128)(2,1)} %gather_fusion, pred[384]{0:T(512)(128)(4,1)S(1)} %get-tuple-element.7), kind=kOutput, calls=%fused_computation.15 | convolution fusion | flops 405798912 | bytes 22022016 | tf_op jit(solution)/shard_map/ksj,sij->ksi/dot_general | solution.py:29
  63.5 4.3 %broadcast_in_dim.28 = f32[32,512,128]{2,0,1:T(8,128)} broadcast(f32[]{:T(128)} %constant.18.clone.1), dimensions={} | broadcast | bytes 8388612 | tf_op jit(solution)/shard_map/broadcast_in_dim | solution.py:35
  67.8 51.2 %scatter_fusion = f32[32,512,128]{2,0,1:T(8,128)} fusion(f32[32,512,128]{2,0,1:T(8,128)} %broadcast_in_dim.28, s32[384]{0:T(512)S(1)} %fusion.21, f32[384,32,128]{2,1,0:T(8,128)} %broadcast_multiply_fusion.1), kind=kCustom, calls=%fused_computation.2 | custom fusion | flops 1572864 | bytes 18875904 | tf_op jit(solution)/shard_map/scatter-add | solution.py:30
  119.1 7.1 %copy_bitcast_fusion = f32[32,65536]{1,0:T(8,128)} fusion(f32[32,512,128]{2,0,1:T(8,128)} %scatter_fusion), kind=kLoop, calls=%fused_computation.8 | loop fusion | bytes 16777216 | tf_op jit(solution)/shard_map/reshape | solution.py:36
  126.2 0.0 copy-start
  126.2 0.0 reduce-scatter.3.cloned.1.call-update
  126.2 0.0 all-gather.5.cloned.1.call-start
  126.3 85.6 %reduce-scatter.3.cloned.1.call-done = f32[32,4096]{1,0:T(8,128)} async-done(((f32[32,65536]{1,0:T(8,128)}), f32[32,4096]{1,0:T(8,128)}) %reduce-scatter.3.cloned.1.call-update) | async-done | bytes 524304 | tf_op jit(solution)/shard_map/reduce_scatter | solution.py:37
  211.8 1.8 convert_element_type.14
  213.6 0.0 all-gather.5.cloned.1.call-update
  213.6 0.2 reduce-scatter.5.cloned.1.call-start
  213.9 0.0 copy-done
  213.9 51.6 %all-gather.5.cloned.1.call-done = bf16[32,65536]{1,0:T(8,128)(2,1)} async-done(((bf16[32,4096]{1,0:T(8,128)(2,1)}), bf16[32,65536]{1,0:T(8,128)(2,1)}) %all-gather.5.cloned.1.call-update) | async-done | bytes 4194320 | tf_op jit(solution)/shard_map/all_gather | solution.py:39
  265.6 4.9 %copy_bitcast_fusion.1 = bf16[32,512,128]{2,0,1:T(8,128)(2,1)} fusion(bf16[32,65536]{1,0:T(8,128)(2,1)} %all-gather.5.cloned.1.call-done), kind=kLoop, calls=%fused_computation.9 | loop fusion | bytes 8388608 | tf_op jit(solution)/shard_map/reshape | solution.py:40
  270.4 3.4 gather_fusion.1
  273.9 9.0 %broadcast_multiply_fusion = f32[384,32,128]{2,1,0:T(8,128)} fusion(f32[384]{0:T(512)S(1)} %get-tuple-element.6, bf16[1,1,384,128,128]{4,3,2,1,0:T(8,128)(2,1)} %param.5, bf16[384,32,128]{2,1,0:T(8,128)(2,1)S(1)} %gather_fusion.1, pred[384]{0:T(512)(128)(4,1)S(1)} %compare_and_fusion), kind=kOutput, calls=%fused_computation.14 | convolution fusion | flops 405798912 | bytes 22022016 | tf_op jit(solution)/shard_map/ksi,sij->ksj/dot_general | solution.py:45
  282.9 2.6 broadcast_in_dim.31
  285.5 51.3 %scatter_fusion.1 = f32[32,256,128]{2,0,1:T(8,128)} fusion(f32[32,256,128]{2,0,1:T(8,128)} %broadcast_in_dim.31, s32[384]{0:T(512)S(1)} %fusion.22, f32[384,32,128]{2,1,0:T(8,128)} %broadcast_multiply_fusion), kind=kCustom, calls=%fused_computation.3 | custom fusion | flops 1572864 | bytes 18875904 | tf_op jit(solution)/shard_map/scatter-add | solution.py:46
  336.8 6.5 %copy.22 = f32[32,256,128]{2,1,0:T(8,128)} copy(f32[32,256,128]{2,0,1:T(8,128)} %scatter_fusion.1) | data formatting | bytes 8388608 | tf_op jit(solution)/shard_map/scatter-add | solution.py:46
  343.3 5.0 %reshape.92 = f32[32,8,1,4096]{3,1,0,2:T(8,128)} reshape(f32[32,256,128]{2,1,0:T(8,128)} %copy.22) | data formatting | bytes 8388608 | tf_op jit(solution)/shard_map/reshape | solution.py:49
  348.3 6.5 %copy.23 = f32[32,8,1,4096]{3,0,2,1:T(8,128)} copy(f32[32,8,1,4096]{3,1,0,2:T(8,128)} %reshape.92) | data formatting | bytes 8388608 | tf_op jit(solution)/shard_map/reshape | solution.py:49
  354.8 0.0 reduce-scatter.5.cloned.1.call-update
  354.9 37.6 %reduce-scatter.5.cloned.1.call-done = f32[32,1,1,4096]{3,0,2,1:T(8,128)} async-done(((f32[32,8,1,4096]{3,0,2,1:T(8,128)}), f32[32,1,1,4096]{3,0,2,1:T(8,128)}) %reduce-scatter.5.cloned.1.call-update) | async-done | bytes 524304 | tf_op jit(solution)/shard_map/reduce_scatter | solution.py:50
  392.5 1.8 convert_element_type.15
  (5 shorter events, 0.0 us)
Async XLA Ops:
  7.2 30.2 %all-gather.3.cloned.1.call-start = ((), (), s32[]{:S(2)}) async-start(), calls=%async_computation.2 | async-start | bytes 2359296 | tf_op jit(solution)/shard_map/all_gather | solution.py:18
  7.9 203.9 %reduce-scatter.3.cloned.1.call-start = ((), (), s32[]{:S(2)}) async-start(), calls=%async_computation.3 | async-start | bytes 8912896 | tf_op jit(solution)/shard_map/reduce_scatter | solution.py:37
  126.2 87.7 %copy-start = (s32[1,1,384]{2,1,0:T(1,128)S(1)}, s32[1,1,384]{2,1,0:T(1,128)}, u32[]{:S(2)}) copy-start(s32[1,1,384]{2,1,0:T(1,128)} %param.6) | copy-start | bytes 4612
  126.2 139.3 %all-gather.5.cloned.1.call-start = ((), (), s32[]{:S(2)}) async-start(), calls=%async_computation.4 | async-start | bytes 4456448 | tf_op jit(solution)/shard_map/all_gather | solution.py:39
  213.6 178.8 %reduce-scatter.5.cloned.1.call-start = ((), (), s32[]{:S(2)}) async-start(), calls=%async_computation.5 | async-start | bytes 4718592 | tf_op jit(solution)/shard_map/reduce_scatter | solution.py:50
Sparse Core Ops, SparseCore 0:
  9.7 27.5 all-gather.2
  126.3 85.4 reduce-scatter.2
  214.6 50.9 all-gather.4
  355.0 37.4 reduce-scatter.4
where the time goes:
time: 402 us; the launch traced here: 401 us
  waiting for transfers between devices  202 us (50%)
  other arithmetic  108 us (27%)
  local copies, waits for them, and re-layouts  51.6 us (13%)
  matrix products  24 us (6%)
  between operations  14.4 us (4%)
    reduce_scatter x1, waiting for transfers between devices, per_device(): lax.psum_scatter(partial_rows, 'col', scatter_dimension=1, tiled=True)  85.6 us
    all_gather x1, waiting for transfers between devices, per_device(): row_image = lax.all_gather(image, 'col', axis=1, tiled=True)  51.6 us
    scatter-add x1, other arithmetic, backward_terms(): return totals.at[:, col_index].add(product * slot_mask[None, :, None])  51.3 us
    scatter-add x1, other arithmetic, forward_terms(): return totals.at[:, row_index].add(product * slot_mask[None, :, None])  51.2 us
    reduce_scatter x1, waiting for transfers between devices, per_device(): lax.psum_scatter(partial_cols, 'row', scatter_dimension=1, tiled=True)  37.6 us
    all_gather x1, waiting for transfers between devices, per_device(): gathered = lax.all_gather(vectors, 'row', axis=1, tiled=True)  26.6 us
    dot_general x1, matrix products, forward_terms(): jnp.einsum('ksj,sij->ksi', picked, tile_block, preferred_element_type=jnp...  14.9 us
    reshape x2, local copies, waits for them, and re-layouts, per_device(): backward_sum.reshape(vec_cols, row_devices, 1, vectors.shape[3])  11.5 us
  transfers between devices with their start and end apart: 4, of which 4 were waited for; matrix products, arithmetic and copies ran while one was open for 1% of the time, Pallas kernels for 0%

commit v1 on v0

--- a/solution.py
+++ b/solution.py
@@ -1,7 +1,18 @@
+import functools
 import jax
 import jax.numpy as jnp
 from jax import lax
 from jax.sharding import PartitionSpec as P
+
+
+def wait_the_figure(mine, device_axis, along_dim):
+    kept_arr = lax.all_to_all(
+        jnp.stack(tuple((mine for _ in range(lax.axis_size(device_axis))))), device_axis, 0, 0
+    )
+    return jnp.concatenate(kept_arr, axis=along_dim)
+
+
+replace_words_for = functools.partial(wait_the_figure, device_axis="col", along_dim=1)
 
 
 def per_device(tiles, tile_row, tile_col, tile_count, vectors):
@@ -36,7 +47,7 @@
     partial_rows = forward_sum.reshape(vec_cols, blk_rows * tile_size)
     share_sum = lax.psum_scatter(partial_rows, "col", scatter_dimension=1, tiled=True)
     image = share_sum.astype(jnp.bfloat16)
-    row_image = lax.all_gather(image, "col", axis=1, tiled=True)
+    row_image = replace_words_for(image)
     row_blocks = row_image.reshape(vec_cols, blk_rows, tile_size)
 
     def backward_terms(totals, start_slot, group_size):

time: 402 us -> 432 us (1.075)
  local copies, waits for them, and re-layouts: 51.6 us -> 69.9 us
  waiting for transfers between devices: 202 us -> 209 us
  starting transfers between devices: 0.34 us -> 5.48 us
    all_to_all x0 -> x1, waiting for transfers between devices: none -> 59.6 us  [wait_the_figure(): lax.all_to_all(jnp.stack(tuple((mine for _ in range(lax.axis_size(device_...]
    all_gather x1 -> x0, waiting for transfers between devices: 51.6 us -> none  [per_device(): row_image = lax.all_gather(image, 'col', axis=1, tiled=True)]
    another operation x0 -> x3, local copies, waits for them, and re-layouts: none -> 16.7 us  [the longest x2 14.3 us: per_device(): row_blocks = row_image.reshape(vec_cols, blk_rows, tile_size)]
    all_to_all x0 -> x1, starting transfers between devices: none -> 5.18 us  [wait_the_figure(): lax.all_to_all(jnp.stack(tuple((mine for _ in range(lax.axis_size(device_...]
  transfers between devices with their start and end apart: 4 -> 4, of which waited for: 4 -> 4; matrix products, arithmetic and copies ran while one was open for 1% -> 0% of each run, Pallas kernels for 0% -> 0%
where the time goes in v1:
time: 432 us; the launch traced here: 430 us
  waiting for transfers between devices  209 us (48%)
  other arithmetic  108 us (25%)
  local copies, waits for them, and re-layouts  69.9 us (16%)
  matrix products  24 us (6%)
  between operations  14.5 us (3%)
  starting transfers between devices  5.48 us (1%)
    reduce_scatter x1, waiting for transfers between devices, per_device(): lax.psum_scatter(partial_rows, 'col', scatter_dimension=1, tiled=True)  85.6 us
    all_to_all x1, waiting for transfers between devices, wait_the_figure(): lax.all_to_all(jnp.stack(tuple((mine for _ in range(lax.axis_size(device_...  59.6 us
    scatter-add x1, other arithmetic, backward_terms(): return totals.at[:, col_index].add(product * slot_mask[None, :, None])  51.3 us
    scatter-add x1, other arithmetic, forward_terms(): return totals.at[:, row_index].add(product * slot_mask[None, :, None])  51.2 us
    reduce_scatter x1, waiting for transfers between devices, per_device(): lax.psum_scatter(partial_cols, 'row', scatter_dimension=1, tiled=True)  36 us
    all_gather x1, waiting for transfers between devices, per_device(): gathered = lax.all_gather(vectors, 'row', axis=1, tiled=True)  26.6 us
    dot_general x1, matrix products, forward_terms(): jnp.einsum('ksj,sij->ksi', picked, tile_block, preferred_element_type=jnp...  14.9 us
    another operation x2, local copies, waits for them, and re-layouts, per_device(): row_blocks = row_image.reshape(vec_cols, blk_rows, tile_size)  14.3 us
  transfers between devices with their start and end apart: 4, of which 4 were waited for; matrix products, arithmetic and copies ran while one was open for 0% of the time, Pallas kernels for 0%

profile of v1, /device:TPU:0, one launch (start us, length us, event | category | flops | bytes accessed | tf_op | source)
XLA Modules:
  0.0 430.0 jit_solution(8558869205527041036)
XLA Ops:
  7.2 0.0 all-gather.2.cloned.1.call-start
  7.2 0.7 all-gather.2.cloned.1.call-update
  7.9 0.0 reduce-scatter.3.cloned.1.call-start
  8.6 0.7 reduce.1
  9.3 0.7 fusion.22
  10.0 0.7 fusion.21
  10.7 26.6 %all-gather.2.cloned.1.call-done = bf16[32,8,1,4096]{3,0,2,1:T(8,128)(2,1)} async-done(((bf16[32,1,1,4096]{3,0,2,1:T(8,128)(2,1)}), bf16[32,8,1,4096]{3,0,2,1:T(8,128)(2,1)}) %all-gather.2.cloned.1.call-update) | async-done | bytes 2097168 | tf_op jit(solution)/shard_map/all_gather | solution.py:29
  37.3 2.7 copy.13
  40.1 2.4 reshape.91
  42.5 2.9 copy.14
  45.4 3.2 gather_fusion
  48.6 14.9 %broadcast_multiply_fusion.1 = f32[384,32,128]{2,1,0:T(8,128)} fusion(f32[384]{0:T(512)S(1)} %get-tuple-element.4, bf16[1,1,384,128,128]{4,3,2,1,0:T(8,128)(2,1)} %param.5, bf16[384,32,128]{2,1,0:T(8,128)(2,1)} %gather_fusion, pred[384]{0:T(512)(128)(4,1)S(1)} %get-tuple-element.5), kind=kOutput, calls=%fused_computation.14 | convolution fusion | flops 405798912 | bytes 22022016 | tf_op jit(solution)/shard_map/ksj,sij->ksi/dot_general | solution.py:40
  63.5 4.3 broadcast_in_dim.28
  67.8 51.2 %scatter_fusion = f32[32,512,128]{2,0,1:T(8,128)} fusion(f32[32,512,128]{2,0,1:T(8,128)} %broadcast_in_dim.28, s32[384]{0:T(512)S(1)} %fusion.21, f32[384,32,128]{2,1,0:T(8,128)} %broadcast_multiply_fusion.1), kind=kCustom, calls=%fused_computation.2 | custom fusion | flops 1572864 | bytes 18875904 | tf_op jit(solution)/shard_map/scatter-add | solution.py:41
  119.1 7.1 %copy_bitcast_fusion = f32[32,65536]{1,0:T(8,128)} fusion(f32[32,512,128]{2,0,1:T(8,128)} %scatter_fusion), kind=kLoop, calls=%fused_computation.8 | loop fusion | bytes 16777216 | tf_op jit(solution)/shard_map/reshape | solution.py:47
  126.2 0.0 reduce-scatter.3.cloned.1.call-update
  126.2 85.6 %reduce-scatter.3.cloned.1.call-done = f32[32,4096]{1,0:T(8,128)} async-done(((f32[32,65536]{1,0:T(8,128)}), f32[32,4096]{1,0:T(8,128)}) %reduce-scatter.3.cloned.1.call-update) | async-done | bytes 524304 | tf_op jit(solution)/shard_map/reduce_scatter | solution.py:48
  211.8 1.1 convert_element_type.14
  212.9 0.0 copy-start
  212.9 2.5 stack.2
  215.4 0.0 copy-start.1
  215.4 0.0 copy-done
  215.4 5.2 %all-to-all-start = ((bf16[16,32,4096]{2,1,0:T(8,128)(2,1)}), bf16[16,32,4096]{2,1,0:T(8,128)(2,1)}, u32[]{:S(2)}, u32[]{:S(2)}) async-start(bf16[16,32,4096]{2,1,0:T(8,128)(2,1)} %stack.2), calls=%async_computation.1 | async-start | bytes 8388608 | tf_op jit(solution)/shard_map/all_to_all | solution.py:9
  220.6 0.2 reduce-scatter.5.cloned.1.call-start
  220.8 0.0 copy-done.1
  220.9 59.6 %all-to-all-done = bf16[16,32,4096]{2,1,0:T(8,128)(2,1)} async-done(((bf16[16,32,4096]{2,1,0:T(8,128)(2,1)}), bf16[16,32,4096]{2,1,0:T(8,128)(2,1)}, u32[]{:S(2)}, u32[]{:S(2)}) %all-to-all-start) | async-done | bytes 4194336 | tf_op jit(solution)/shard_map/all_to_all | solution.py:9
  280.5 6.5 %copy.16 = bf16[32,16,4096]{2,1,0:T(8,128)(2,1)} copy(bf16[32,16,4096]{2,0,1:T(8,128)(2,1)} %bitcast.5) | data formatting | bytes 8388608 | tf_op jit(solution)/shard_map/reshape | solution.py:12
  287.0 7.4 %reshape_reshape.3 = bf16[32,512,128]{2,1,0:T(8,128)(2,1)} reshape(bf16[32,16,4096]{2,1,0:T(8,128)(2,1)} %copy.16) | data formatting | bytes 8388608 | tf_op jit(solution)/shard_map/reshape;reshape | solution.py:51
  294.4 6.9 %copy.17 = bf16[32,512,128]{2,0,1:T(8,128)(2,1)} copy(bf16[32,512,128]{2,1,0:T(8,128)(2,1)} %reshape_reshape.3) | data formatting | bytes 8388608 | tf_op jit(solution)/shard_map/reshape;reshape | solution.py:51
  301.2 3.4 gather_fusion.1
  304.7 9.0 %broadcast_multiply_fusion = f32[384,32,128]{2,1,0:T(8,128)} fusion(f32[384]{0:T(512)S(1)} %get-tuple-element.4, bf16[1,1,384,128,128]{4,3,2,1,0:T(8,128)(2,1)} %param.5, bf16[384,32,128]{2,1,0:T(8,128)(2,1)S(1)} %gather_fusion.1, pred[384]{0:T(512)(128)(4,1)S(1)} %compare_and_fusion), kind=kOutput, calls=%fused_computation.13 | convolution fusion | flops 405798912 | bytes 22022016 | tf_op jit(solution)/shard_map/ksi,sij->ksj/dot_general | solution.py:56
  313.7 2.6 broadcast_in_dim.31
  316.3 51.3 %scatter_fusion.1 = f32[32,256,128]{2,0,1:T(8,128)} fusion(f32[32,256,128]{2,0,1:T(8,128)} %broadcast_in_dim.31, s32[384]{0:T(512)S(1)} %fusion.22, f32[384,32,128]{2,1,0:T(8,128)} %broadcast_multiply_fusion), kind=kCustom, calls=%fused_computation.3 | custom fusion | flops 1572864 | bytes 18875904 | tf_op jit(solution)/shard_map/scatter-add | solution.py:57
  367.6 6.5 %copy.18 = f32[32,256,128]{2,1,0:T(8,128)} copy(f32[32,256,128]{2,0,1:T(8,128)} %scatter_fusion.1) | data formatting | bytes 8388608 | tf_op jit(solution)/shard_map/scatter-add | solution.py:57
  374.1 5.0 %reshape.94 = f32[32,8,1,4096]{3,1,0,2:T(8,128)} reshape(f32[32,256,128]{2,1,0:T(8,128)} %copy.18) | data formatting | bytes 8388608 | tf_op jit(solution)/shard_map/reshape | solution.py:60
  379.1 6.5 %copy.19 = f32[32,8,1,4096]{3,0,2,1:T(8,128)} copy(f32[32,8,1,4096]{3,1,0,2:T(8,128)} %reshape.94) | data formatting | bytes 8388608 | tf_op jit(solution)/shard_map/reshape | solution.py:60
  385.6 0.0 reduce-scatter.5.cloned.1.call-update
  385.6 36.0 %reduce-scatter.5.cloned.1.call-done = f32[32,1,1,4096]{3,0,2,1:T(8,128)} async-done(((f32[32,8,1,4096]{3,0,2,1:T(8,128)}), f32[32,1,1,4096]{3,0,2,1:T(8,128)}) %reduce-scatter.5.cloned.1.call-update) | async-done | bytes 524304 | tf_op jit(solution)/shard_map/reduce_scatter | solution.py:61
  421.7 1.8 convert_element_type.15
  (5 shorter events, 0.0 us)
Async XLA Ops:
  7.2 30.2 %all-gather.2.cloned.1.call-start = ((), (), s32[]{:S(2)}) async-start(), calls=%async_computation.3 | async-start | bytes 2359296 | tf_op jit(solution)/shard_map/all_gather | solution.py:29
  7.9 203.9 %reduce-scatter.3.cloned.1.call-start = ((), (), s32[]{:S(2)}) async-start(), calls=%async_computation.4 | async-start | bytes 8912896 | tf_op jit(solution)/shard_map/reduce_scatter | solution.py:48
  212.9 2.5 copy-start
  215.4 5.4 %copy-start.1 = (s32[1,1,384]{2,1,0:T(1,128)S(1)}, s32[1,1,384]{2,1,0:T(1,128)}, u32[]{:S(2)}) copy-start(s32[1,1,384]{2,1,0:T(1,128)} %param.6) | copy-start | bytes 4612
  215.4 65.1 %all-to-all-start = ((bf16[16,32,4096]{2,1,0:T(8,128)(2,1)}), bf16[16,32,4096]{2,1,0:T(8,128)(2,1)}, u32[]{:S(2)}, u32[]{:S(2)}) async-start(bf16[16,32,4096]{2,1,0:T(8,128)(2,1)} %stack.2), calls=%async_computation.1 | async-start | bytes 8388608 | tf_op jit(solution)/shard_map/all_to_all | solution.py:9
  220.6 201.1 %reduce-scatter.5.cloned.1.call-start = ((), (), s32[]{:S(2)}) async-start(), calls=%async_computation.5 | async-start | bytes 4718592 | tf_op jit(solution)/shard_map/reduce_scatter | solution.py:61
Sparse Core Ops, SparseCore 0:
  9.7 27.5 all-gather.1
  126.3 85.4 reduce-scatter.2
  385.8 35.8 reduce-scatter.4
